TPU v7x, 32 devices: a whole 2x2x4 slice. The times are simulated.
32 devices in a mesh: tx: 4 (over y, x), ty: 2 (over core), depth: 4 (over z).
Axes of the slice: x: 2, y: 2, z: 4, core: 2. Of those that a mesh axis runs over, the one named last changes fastest.
Arguments:
- volume: bfloat16 [128, 512, 512], P('depth', 'ty', 'tx'), may hold values from -6 to 6
- transfer: float32 [4, 2], replicated, may hold values from -1.5 to 1.5
- ray_start: int32 [4, 512, 512], P('depth', 'ty', 'tx'), may hold values from 0 to 15
- ray_stop: int32 [4, 512, 512], P('depth', 'ty', 'tx'), may hold values from 16 to 32
- pattern: int32 [4, 64, 4], P('depth', 'ty', 'tx'), may hold values 0 or 1
- depth_order: int32 [4], replicated, may hold values from 0 to 3, each once
Outputs:
- frame: float32 [4, 512, 512], P(None, 'ty', 'tx')
Inputs may be any that keep to these rules, and one draw needn't show every extreme that they name: ray_start[s] < ray_stop[s] for every ray and slice. `depth_order`: each slice appears once.
All inputs are finite; a program needn't handle non-finite values. No bound on the sum of `pattern` on one device may be relied on, other than what follows from the above.
Results may differ from a plain program's by a relative error of at most 0.0003.
Values may be sent and summed in bfloat16 or wider, within the bound.
A program may use at most 64 MiB of HBM per device.

v0:
```python
import functools
import math

import jax
import jax.numpy as jnp
from jax import lax
from jax.experimental import pallas as pl
from jax.experimental.pallas import tpu as pltpu
from jax.sharding import PartitionSpec as P

MESH = pl.DeviceIdType.MESH
STRIP = 16
LAG_ROWS = 224
UNROLL = 32
LOG2E = math.log2(math.e)
OCTAVES = 22
CODES = 65535.0 / OCTAVES


def encode(x):
    place = jnp.log(jnp.clip(x, 1e-30, 1.0)) * (CODES * LOG2E) + 65535.5
    return (jnp.maximum(place, 0.0).astype(jnp.int32) - 32768).astype(jnp.int16)


def decode(code):
    wide = code.astype(jnp.int32)
    value = jnp.exp2((wide.astype(jnp.float32) - 32767.0) * (1.0 / CODES))
    return jnp.where(wide == -32768, 0.0, value)


def dot(a, b):
    return jnp.dot(a, b, preferred_element_type=jnp.float32)


def kernel(
    n, n_tx, n_ty, scale, each,
    vol, start_hbm, stop_hbm, pattern, transfer, order, out,
    vb, start, stop, yup, ydn, edge, xl, xr, vf, share, held, part, parts, fin,
    load_sem, halo_send, halo_recv, part_send, part_recv, fin_send, fin_recv,
):
    samples, ny, nx = vol.shape
    half = ny // 2
    chunks = ny // each
    lag = LAG_ROWS // each
    tx, ty, me = lax.axis_index("tx"), lax.axis_index("ty"), lax.axis_index("depth")

    loads = [
        pltpu.make_async_copy(vol, vb.at[pl.ds(1, samples)], load_sem.at[0]),
        pltpu.make_async_copy(start_hbm.at[0], start, load_sem.at[1]),
        pltpu.make_async_copy(stop_hbm.at[0], stop, load_sem.at[2]),
    ]
    for load in loads:
        load.start()

    barrier = pltpu.get_barrier_semaphore()
    for rel in range(1, n):
        pl.semaphore_signal(barrier, inc=1, device_id={"depth": lax.rem(me + rel, n)}, device_id_type=MESH)
    sides = (("tx", tx, n_tx), ("ty", ty, n_ty))
    expected = n - 1
    for axis, at, count in sides:
        @pl.when(at > 0)
        def _(axis=axis, at=at):
            pl.semaphore_signal(barrier, inc=1, device_id={axis: at - 1}, device_id_type=MESH)

        @pl.when(at < count - 1)
        def _(axis=axis, at=at):
            pl.semaphore_signal(barrier, inc=1, device_id={axis: at + 1}, device_id_type=MESH)

        expected = expected + jnp.where(at > 0, 1, 0) + jnp.where(at < count - 1, 1, 0)
    pl.semaphore_wait(barrier, expected)

    def shift(slot, axis, at, count, source, target, upward):
        return pltpu.make_async_remote_copy(
            src_ref=source, dst_ref=target, send_sem=halo_send.at[slot], recv_sem=halo_recv.at[slot],
            device_id={axis: at + 1 if upward else at - 1}, device_id_type=MESH,
        )

    last, first = pl.ds(ny - STRIP, STRIP), pl.ds(0, STRIP)
    halos = [
        (shift(0, "depth", me, n, vb.at[samples], vb.at[0], True), me, n, True, lambda: vb.at[0]),
        (shift(1, "depth", me, n, vb.at[1], vb.at[samples + 1], False), me, n, False, lambda: vb.at[samples + 1]),
        (shift(2, "ty", ty, n_ty, vb.at[pl.ds(1, samples), last], yup, True), ty, n_ty, True, lambda: yup),
        (shift(3, "ty", ty, n_ty, vb.at[pl.ds(1, samples), first], ydn, False), ty, n_ty, False, lambda: ydn),
        (shift(4, "tx", tx, n_tx, edge, xl, True), tx, n_tx, True, lambda: xl),
        (shift(5, "tx", tx, n_tx, edge, xr, False), tx, n_tx, False, lambda: xr),
    ]

    def send_halo(entry):
        copy, at, count, upward, place = entry
        pl.when(at < count - 1 if upward else at > 0)(copy.start)

        @pl.when(at == 0 if upward else at == count - 1)
        def _():
            place()[...] = jnp.zeros(place().shape, jnp.bfloat16)

    loads[0].wait()
    for entry in halos[:4]:
        send_halo(entry)

    group = 4
    r = lax.broadcasted_iota(jnp.int32, (nx, nx), 0)
    c = lax.broadcasted_iota(jnp.int32, (nx, nx), 1)

    def gather(step, total):
        z0 = step * group
        hits = []
        for k in range(group):
            lane = 2 * (z0 + k)
            hit = ((r == nx - 1) & (c == lane)) | ((r == 0) & (c == lax.rem(lane + nx - 1, nx)))
            hits.append(hit.astype(jnp.float32).astype(jnp.bfloat16))
        layers = jnp.concatenate([vb[1 + z0 + k] for k in range(group)], axis=1)
        return total + dot(layers, jnp.concatenate(hits, axis=0))

    columns = lax.fori_loop(0, samples // group, gather, jnp.zeros((ny, nx), jnp.float32))
    edge[...] = (columns[:half] + pltpu.roll(columns[half:], nx // 2, 1)).astype(jnp.bfloat16)
    for entry in halos[4:]:
        send_halo(entry)

    body = pl.ds(8, ny)

    loads[1].wait()
    loads[2].wait()
    rows_each = ny // pattern.shape[1]
    slopes = [transfer[0, i] * 0.5 for i in range(3)]
    offsets = [transfer[1, i] * 0.5 for i in range(3)]
    slope, offset = transfer[0, 3] * LOG2E, transfer[1, 3] * LOG2E

    rank = [sum(jnp.where(order[q] == s, q, 0) for q in range(n)) for s in range(n)]
    before = [[jnp.where(rank[a] < rank[b], 1.0, 0.0) for b in range(n)] for a in range(n)]

    def owner_of(j):
        turn = lax.rem(j, n)
        return jnp.where(lax.rem(turn, 2) == 0, turn // 2, n - 1 - turn // 2)

    @pl.loop(0, chunks)
    def _(j):
        r0 = pl.multiple_of(j * each, each)
        rows, inner = pl.ds(r0, each), pl.ds(pl.multiple_of(r0 + 8, 8), each)
        begin = start[rows]
        end = stop[rows]
        blocks = []
        for b in range(each // rows_each):
            on = pattern[0, j * (each // rows_each) + b]
            blocks.append(jnp.where(on > 0, end[b * rows_each:(b + 1) * rows_each], 0))
        end = jnp.concatenate(blocks, axis=0)

        def layer(z, passed):
            v = vb[z + 1, rows].astype(jnp.float32)
            vf[z + 1, inner] = v
            log = jnp.log(1.0 + jnp.exp2(v * slope + offset))
            through = jnp.exp2(log * (-scale * LOG2E))
            active = (begin <= z) & (end > z)
            now = jnp.where(active, passed * through, passed)
            share[z, rows] = passed - now
            return now

        passed = lax.fori_loop(0, samples, layer, jnp.ones((each, nx), jnp.float32), unroll=UNROLL)
        hidden = encode(1.0 - passed)
        owner, k = owner_of(j), j // n

        @pl.when(owner == me)
        def _():
            parts[me, k, 3] = hidden

        @pl.when(owner != me)
        def _():
            part[j, 3] = hidden

    for copy, at, count, upward, place in halos:
        pl.when(at < count - 1 if upward else at > 0)(copy.wait_send)
        pl.when(at > 0 if upward else at < count - 1)(copy.wait_recv)

    lane = lax.broadcasted_iota(jnp.int32, (half, nx), 1)
    held[...] = jnp.where(lax.rem(lane, 2) == 0, xl[...].astype(jnp.float32), xr[...].astype(jnp.float32))
    for z in (0, samples + 1):
        vf[z, body] = vb[z].astype(jnp.float32)

    @pl.loop(0, samples)
    def _(z):
        vf[1 + z, pl.ds(0, 8)] = yup[z].astype(jnp.float32)[STRIP - 8:]
        vf[1 + z, pl.ds(8 + ny, 8)] = ydn[z].astype(jnp.float32)[:8]

    def part_copy(j, k, owner):
        return pltpu.make_async_remote_copy(
            src_ref=part.at[j], dst_ref=parts.at[me, k],
            send_sem=part_send.at[j], recv_sem=part_recv.at[me, k],
            device_id={"depth": owner}, device_id_type=MESH,
        )

    def fin_copy(j, k, rel):
        return pltpu.make_async_remote_copy(
            src_ref=fin.at[k], dst_ref=out.at[:, pl.ds(pl.multiple_of(j * each, each), each)],
            send_sem=fin_send.at[k, rel - 1], recv_sem=fin_recv.at[j],
            device_id={"depth": lax.rem(me + rel, n)}, device_id_type=MESH,
        )

    def render(j):
        r0 = pl.multiple_of(j * each, each)
        rows = pl.ds(r0, each)
        def layer(z, state):
            previous, v, total, red, green, blue = state
            after = vf[z + 2, pl.ds(pl.multiple_of(r0 + 8, 8), each)]
            near = vf.at[z + 1, pl.ds(r0, each + 16)]
            dz = after - previous
            dyv = near[pl.ds(9, each)] - near[pl.ds(7, each)]
            beside = pltpu.roll(sides_of, lax.rem(nx - 2 * z, nx), 1)
            right = jnp.where(lane == nx - 1, beside, pltpu.roll(v, nx - 1, 1))
            dxv = right - jnp.where(lane == 0, beside, pltpu.roll(v, 1, 1))
            lit = jnp.abs(0.168 * dxv + 0.21 * dyv + 0.224 * dz)
            shade = 0.15 + lit * lax.rsqrt(dxv * dxv + dyv * dyv + dz * dz + 4.0)
            weight = share[z, rows] * shade
            tints = [jnp.tanh(v * slopes[i] + offsets[i]) for i in range(3)]
            return (
                v, after, total + weight,
                red + weight * tints[0], green + weight * tints[1], blue + weight * tints[2],
            )

        upper = j * each // half
        sides_of = held[pl.ds(pl.multiple_of(r0 - upper * half, each), each)]
        sides_of = pltpu.roll(sides_of, upper * (nx // 2), 1)
        lane = lax.broadcasted_iota(jnp.int32, (each, nx), 1)
        zero = jnp.zeros((each, nx), jnp.float32)
        inner = pl.ds(pl.multiple_of(r0 + 8, 8), each)
        state = (
            vf[0, inner], vf[1, inner],
            zero, zero, zero, zero,
        )
        _, _, total, red, green, blue = lax.fori_loop(0, samples, layer, state, unroll=UNROLL)
        values = [encode(x) for x in (red + total, green + total, blue + total)]
        owner, k = owner_of(j), j // n

        @pl.when(owner == me)
        def _():
            for i in range(3):
                parts[me, k, i] = values[i]

        @pl.when(owner != me)
        def _():
            for i in range(3):
                part[j, i] = values[i]
            part_copy(j, k, owner).start()

    def merge(j):
        owner, k = owner_of(j), j // n

        @pl.when(owner == me)
        def _():
            for rel in range(1, n):
                source = lax.rem(me + rel, n)
                pltpu.make_async_remote_copy(
                    src_ref=part.at[j], dst_ref=parts.at[source, k],
                    send_sem=part_send.at[j], recv_sem=part_recv.at[source, k],
                    device_id={"depth": source}, device_id_type=MESH,
                ).wait_recv()
            hidden = [decode(parts[s, k, 3]) for s in range(n)]
            remain = 1.0 - hidden[0]
            for s in range(1, n):
                remain = remain * (1.0 - hidden[s])
            colors = [jnp.zeros_like(remain)] * 3
            for s in range(n):
                prefix = jnp.ones_like(remain)
                for a in range(n):
                    if a != s:
                        prefix = prefix * (1.0 - hidden[a] * before[a][s])
                colors = [colors[i] + prefix * decode(parts[s, k, i]) for i in range(3)]
            rows = pl.ds(pl.multiple_of(j * each, each), each)
            for i, value in enumerate(colors + [1.0 - remain]):
                fin[k, i] = encode(value)
                out[i, rows] = encode(value)
            for rel in range(1, n):
                fin_copy(j, k, rel).start()

    @pl.loop(0, chunks + lag)
    def _(j):
        pl.when(j < chunks)(lambda: render(j))
        pl.when(j >= lag)(lambda: merge(j - lag))

    @pl.loop(0, chunks)
    def _(j):
        owner, k = owner_of(j), j // n

        @pl.when(owner == me)
        def _():
            for rel in range(1, n):
                fin_copy(j, k, rel).wait_send()

        @pl.when(owner != me)
        def _():
            part_copy(j, k, owner).wait_send()
            fin_copy(j, k, 1).wait_recv()


def solution(mesh):
    n, n_tx, n_ty = mesh.shape["depth"], mesh.shape["tx"], mesh.shape["ty"]

    def shards(volume, transfer, ray_start, ray_stop, pattern, depth_order):
        samples, ny, nx = volume.shape
        rows = min(32, ny // n)
        chunks = ny // rows
        owned = chunks // n
        f32, bf16, i16 = jnp.float32, jnp.bfloat16, jnp.int16
        any_space = pl.BlockSpec(memory_space=pl.ANY)
        smem = pl.BlockSpec(memory_space=pltpu.SMEM)
        dma = pltpu.SemaphoreType.DMA
        codes = pl.pallas_call(
            functools.partial(kernel, n, n_tx, n_ty, 2.0 / (samples * n), rows),
            out_shape=jax.ShapeDtypeStruct((4, ny, nx), i16),
            in_specs=[any_space, any_space, any_space, smem, smem, smem],
            out_specs=pl.BlockSpec(memory_space=pltpu.VMEM),
            scratch_shapes=[
                pltpu.VMEM((samples + 2, ny, nx), bf16),
                pltpu.VMEM((ny, nx), jnp.int32),
                pltpu.VMEM((ny, nx), jnp.int32),
                pltpu.VMEM((samples, STRIP, nx), bf16),
                pltpu.VMEM((samples, STRIP, nx), bf16),
                pltpu.VMEM((ny // 2, nx), bf16),
                pltpu.VMEM((ny // 2, nx), bf16),
                pltpu.VMEM((ny // 2, nx), bf16),
                pltpu.VMEM((samples + 2, ny + 16, nx), f32),
                pltpu.VMEM((samples, ny, nx), f32),
                pltpu.VMEM((ny // 2, nx), f32),
                pltpu.VMEM((chunks, 4, rows, nx), i16),
                pltpu.VMEM((n, owned, 4, rows, nx), i16),
                pltpu.VMEM((owned, 4, rows, nx), i16),
                dma((3,)), dma((6,)), dma((6,)),
                dma((chunks,)), dma((n, owned)), dma((owned, n - 1)), dma((chunks,)),
            ],
            compiler_params=pltpu.CompilerParams(
                collective_id=0, has_side_effects=True, vmem_limit_bytes=62 * 1024 * 1024
            ),
        )(volume, ray_start, ray_stop, pattern[:, :, 0], transfer.T, depth_order)
        return decode(codes)

    in_specs = (
        P("depth", "ty", "tx"),
        P(),
        P("depth", "ty", "tx"),
        P("depth", "ty", "tx"),
        P("depth", "ty", "tx"),
        P(),
    )
    return jax.shard_map(shards, mesh=mesh, in_specs=in_specs, out_specs=P(None, "ty", "tx"), check_vma=False)
```

profile of v0, /device:TPU:0, one launch (start us, length us, event | category | flops | bytes accessed | tf_op | source)
XLA Modules:
  0.0 28.0 jit_solution(15075878233596683155)
XLA Ops:
  0.0 26.0 %shard_map.64 = s16[4,256,128]{2,1,0:T(8,128)(2,1)} custom-call(bf16[32,256,128]{2,1,0:T(8,128)(2,1)} %vol.1, s32[1,256,128]{2,1,0:T(8,128)} %start_hbm.1, s32[1,256,128]{2,1,0:T(8,128)} %stop_hbm.1, s32[1,32]{1,0:T(1,128)} %bitcast.3, f32[2,4]{1,0:T(2,128)} %bitcast.2, s32[4]{0:T(128)} %order.1), custom_call_target="tpu_custom_call" | custom-call | tf_op jit(solution)/shard_map/pallas_call | solution.py:305
  26.0 1.9 %fusion.3 = f32[4,256,128]{2,1,0:T(8,128)} fusion(s16[4,256,128]{2,1,0:T(8,128)(2,1)} %shard_map.64), kind=kLoop, calls=%fused_computation.5 | loop fusion | flops 786432 | bytes 786432 | tf_op jit(solution)/shard_map/jit(_where)/select_n | solution.py:28
where the time goes:
time: 28.1 us; the launch traced here: 28 us
  Pallas kernels  26 us (93%)
  other arithmetic  1.92 us (7%)
    pallas_call x1, Pallas kernels, shards(): pl.pallas_call(functools.partial(kernel, n, n_tx, n_ty, 2.0 / (samples *...  26 us
    select_n x1, other arithmetic, decode(): return jnp.where(wide == -32768, 0.0, value)  1.92 us

commit v1 on v0

v1 whole, which is shorter than its diff:
```python
import functools
import math

import jax
import jax.numpy as jnp
from jax import lax
from jax.experimental import pallas as pl
from jax.experimental.pallas import tpu as pltpu
from jax.sharding import PartitionSpec as P

MESH = pl.DeviceIdType.MESH
STRIP = 16
UNROLL = 32
LOG2E = math.log2(math.e)
OCTAVES = 24
CODES = 65535.0 / OCTAVES
LEVELS = 65000.0
MERGE_LAG = 4
RELAY_LAG = 7
HIDE_LAG = 3


def encode(x):
    place = jnp.log(jnp.clip(x, 1e-30, 1.0)) * (CODES * LOG2E) + 65535.5
    return (jnp.maximum(place, 0.0).astype(jnp.int32) - 32768).astype(jnp.int16)


def decode(code):
    wide = code.astype(jnp.int32)
    value = jnp.exp2((wide.astype(jnp.float32) - 32767.0) * (1.0 / CODES))
    return jnp.where(wide == -32768, 0.0, value)


def to_level(x):
    return (jnp.minimum(x + 0.5, 65535.0).astype(jnp.int32) - 32768).astype(jnp.int16)


def from_level(code):
    return code.astype(jnp.int32).astype(jnp.float32) + 32768.0


def kernel(
    n, n_tx, n_ty, scale, each,
    vol, start_hbm, stop_hbm, pattern, transfer, order, out,
    vb, start, stop, yup, ydn, edge, xl, xr, vf, share,
    hide, hides, part, parts, factor,
    load_sem, halo_send, halo_recv, edge_send, edge_recv, far,
    hide_send, hide_recv, part_send, part_recv, fin_send, fin_recv, top_send, top_recv,
):
    samples, ny, nx = vol.shape
    chunks = ny // each
    group = 2 * each
    last_chunk = chunks - 1
    second = last_chunk // 2
    slots = last_chunk - second + 1
    tx, ty, me = lax.axis_index("tx"), lax.axis_index("ty"), lax.axis_index("depth")

    def rows_of(j):
        return pl.ds(pl.multiple_of(j * each, each), each)

    def owner_of(j):
        return jnp.where(j < second, n // 2, n // 2 - 1)

    def slot_of(j):
        return jnp.where(j < second, j, jnp.where(j == last_chunk, slots - 1, j - second))

    def load_piece(j):
        return pltpu.make_async_copy(
            vol.at[:, rows_of(j)], vb.at[pl.ds(1, samples), rows_of(j)], load_sem.at[j]
        )

    loads = [
        pltpu.make_async_copy(start_hbm.at[0], start, load_sem.at[chunks]),
        pltpu.make_async_copy(stop_hbm.at[0], stop, load_sem.at[chunks + 1]),
    ]
    barrier = pltpu.get_barrier_semaphore()
    sides = (("tx", tx, n_tx), ("ty", ty, n_ty), ("depth", me, n))
    expected = 0
    for axis, at, count in sides:
        @pl.when(at > 0)
        def _(axis=axis, at=at):
            pl.semaphore_signal(barrier, inc=1, device_id={axis: at - 1}, device_id_type=MESH)

        @pl.when(at < count - 1)
        def _(axis=axis, at=at):
            pl.semaphore_signal(barrier, inc=1, device_id={axis: at + 1}, device_id_type=MESH)

        expected = expected + jnp.where(at > 0, 1, 0) + jnp.where(at < count - 1, 1, 0)

    load_piece(0).start()
    for load in loads:
        load.start()
    for j in range(1, chunks):
        load_piece(j).start()
    pl.semaphore_wait(barrier, expected)

    def far_signal(r):
        @pl.when((me - r + 1 >= 0) & (me + 1 < n))
        def _():
            pl.semaphore_signal(far.at[r, 0], inc=1, device_id={"depth": me + 1}, device_id_type=MESH)

        @pl.when((me + r - 1 < n) & (me - 1 >= 0))
        def _():
            pl.semaphore_signal(far.at[r, 1], inc=1, device_id={"depth": me - 1}, device_id_type=MESH)

    def far_wait(r):
        @pl.when(me - r >= 0)
        def _():
            pl.semaphore_wait(far.at[r, 0], 1)

        @pl.when(me + r < n)
        def _():
            pl.semaphore_wait(far.at[r, 1], 1)

        if r + 1 < n:
            far_signal(r + 1)

    def shift(sems, slot, axis, at, source, target, upward):
        return pltpu.make_async_remote_copy(
            src_ref=source, dst_ref=target, send_sem=sems[0].at[slot], recv_sem=sems[1].at[slot],
            device_id={axis: at + 1 if upward else at - 1}, device_id_type=MESH,
        )

    halo = (halo_send, halo_recv)
    last, first = pl.ds(ny - STRIP, STRIP), pl.ds(0, STRIP)
    halos = [
        (shift(halo, 2, "ty", ty, vol.at[:, last], yup, True), ty, n_ty, True, lambda: yup),
        (shift(halo, 3, "ty", ty, vol.at[:, first], ydn, False), ty, n_ty, False, lambda: ydn),
        (shift(halo, 0, "depth", me, vol.at[samples - 1], vb.at[0], True), me, n, True, lambda: vb.at[0]),
        (shift(halo, 1, "depth", me, vol.at[0], vb.at[samples + 1], False), me, n, False, lambda: vb.at[samples + 1]),
    ]

    def edge_copies(g):
        rows = pl.ds(pl.multiple_of(g * group, group), group)
        sems = (edge_send, edge_recv)
        return [
            (shift(sems, 2 * g, "tx", tx, edge.at[rows], xl.at[rows], True), tx, n_tx, True, None),
            (shift(sems, 2 * g + 1, "tx", tx, edge.at[rows], xr.at[rows], False), tx, n_tx, False, None),
        ]

    def send_halo(entry):
        copy, at, count, upward, place = entry
        pl.when(at < count - 1 if upward else at > 0)(copy.start)
        if place is not None:
            @pl.when(at == 0 if upward else at == count - 1)
            def _():
                place()[...] = jnp.zeros(place().shape, jnp.bfloat16)

    def wait_sent(entry):
        copy, at, count, upward, _ = entry
        pl.when(at < count - 1 if upward else at > 0)(copy.wait_send)

    def wait_arrived(entry):
        copy, at, count, upward, _ = entry
        pl.when(at > 0 if upward else at < count - 1)(copy.wait_recv)

    for entry in halos:
        send_halo(entry)
    if n > 2:
        far_signal(2)

    for at, count, place in ((tx, 0, xl), (tx, n_tx - 1, xr)):
        @pl.when(at == count)
        def _(place=place):
            place[...] = jnp.zeros(place.shape, jnp.bfloat16)

    rows_each = ny // pattern.shape[1]
    slopes = [transfer[0, i] * 0.5 for i in range(3)]
    offsets = [transfer[1, i] * 0.5 for i in range(3)]
    slope, offset = transfer[0, 3] * LOG2E, transfer[1, 3] * LOG2E

    rank = [sum(jnp.where(order[q] == s, q, 0) for q in range(n)) for s in range(n)]
    before = [[jnp.where(rank[a] < rank[b], 1.0, 0.0) for b in range(n)] for a in range(n)]
    lane = lax.broadcasted_iota(jnp.int32, (each, nx), 1)
    pair = lax.shift_right_arithmetic(lane, 1)

    for load in loads:
        load.wait()

    @pl.loop(0, chunks)
    def _(j):
        load_piece(j).wait()
        r0 = pl.multiple_of(j * each, each)
        rows, inner = rows_of(j), pl.ds(pl.multiple_of(r0 + 8, 8), each)
        begins, ends = [], []
        for b in range(each // rows_each):
            on = pattern[0, j * (each // rows_each) + b] > 0
            block = pl.ds(pl.multiple_of(r0 + b * rows_each, rows_each), rows_each)
            begins.append(jnp.where(on, start[block], samples))
            ends.append(jnp.where(on, stop[block], 0))
        begin, end = jnp.concatenate(begins, axis=0), jnp.concatenate(ends, axis=0)

        def layer(early, z, state):
            passed, edges = state
            v = vb[z + 1, rows].astype(jnp.float32)
            vf[z + 1, inner] = v
            edges = jnp.where(pair == z, pltpu.roll(v, lax.rem(2 * z + 1, nx), 1), edges)
            log = jnp.log(1.0 + jnp.exp2(v * slope + offset))
            through = jnp.exp2(log * (-scale * LOG2E))
            now = jnp.where(begin <= z if early else end > z, passed * through, passed)
            share[z, rows] = passed - now
            return now, edges

        state = (jnp.ones((each, nx), jnp.float32), jnp.zeros((each, nx), jnp.float32))
        state = lax.fori_loop(0, samples // 2, functools.partial(layer, True), state, unroll=UNROLL // 2)
        passed, edges = lax.fori_loop(samples // 2, samples, functools.partial(layer, False), state, unroll=UNROLL // 2)
        edge[rows] = edges.astype(jnp.bfloat16)
        hide[j] = encode(1.0 - passed)

        @pl.when(lax.rem(j, 2) == 1)
        def _():
            for entry in edge_copies(j // 2):
                send_halo(entry)

    def to_merger(source, target, sends, recvs, j, dest):
        return pltpu.make_async_remote_copy(
            src_ref=source.at[j], dst_ref=target.at[me, slot_of(j)],
            send_sem=sends.at[j, lax.rem(dest + n - me, n)], recv_sem=recvs.at[me, slot_of(j)],
            device_id={"depth": dest}, device_id_type=MESH,
        )

    def hide_copy(j, dest):
        return to_merger(hide, hides, hide_send, hide_recv, j, dest)

    def part_copy(j, dest):
        return to_merger(part, parts, part_send, part_recv, j, dest)

    def wait_from(source, target, sends, recvs, j):
        for rel in range(1, n):
            other = lax.rem(me + rel, n)
            pltpu.make_async_remote_copy(
                src_ref=source.at[j], dst_ref=target.at[other, slot_of(j)],
                send_sem=sends.at[j, rel], recv_sem=recvs.at[other, slot_of(j)],
                device_id={"depth": other}, device_id_type=MESH,
            ).wait_recv()

    def send_to_merger(copy, source, target, j):
        owner = owner_of(j)

        @pl.when(owner == me)
        def _():
            target[me, slot_of(j)] = source[j]

        @pl.when(owner != me)
        def _():
            copy(j, owner).start()

    def send_to_all(copy, source, target):
        target[me, slots - 1] = source[last_chunk]
        for rel in range(1, n):
            copy(last_chunk, lax.rem(me + rel, n)).start()

    def top_copy(j, right):
        return pltpu.make_async_remote_copy(
            src_ref=out.at[3, rows_of(j)], dst_ref=out.at[3, rows_of(j)],
            send_sem=top_send.at[j, 1 if right else 0], recv_sem=top_recv.at[j],
            device_id={"depth": me + 1 if right else me - 1}, device_id_type=MESH,
        )

    def fin_copy(j, right):
        return pltpu.make_async_remote_copy(
            src_ref=out.at[pl.ds(0, 3), rows_of(j)], dst_ref=out.at[pl.ds(0, 3), rows_of(j)],
            send_sem=fin_send.at[j, 1 if right else 0], recv_sem=fin_recv.at[j],
            device_id={"depth": me + 1 if right else me - 1}, device_id_type=MESH,
        )

    def spread(copy, j, act):
        owner = owner_of(j)
        pl.when((me >= owner) & (me < n - 1))(lambda: act(copy(j, True)))
        pl.when((me <= owner) & (me > 0))(lambda: act(copy(j, False)))

    def relay(copy, j):
        @pl.when(owner_of(j) != me)
        def _():
            copy(j, True).wait_recv()
            spread(copy, j, lambda c: c.start())

    for r in range(2, max(3, n // 2 + 1)):
        if r < n:
            far_wait(r)

    @pl.loop(0, last_chunk)
    def _(j):
        send_to_merger(hide_copy, hide, hides, j)

    for entry in halos:
        wait_arrived(entry)

    @pl.loop(0, samples, unroll=4)
    def _(z):
        vf[1 + z, pl.ds(0, 8)] = yup[z].astype(jnp.float32)[STRIP - 8:]
        vf[1 + z, pl.ds(8 + ny, 8)] = ydn[z].astype(jnp.float32)[:8]

    def render(j):
        r0 = pl.multiple_of(j * each, each)
        rows, inner = rows_of(j), pl.ds(pl.multiple_of(r0 + 8, 8), each)

        @pl.when(lax.rem(j, 2) == 0)
        def _():
            for entry in edge_copies(j // 2):
                wait_arrived(entry)

        vf[samples + 1, inner] = vb[samples + 1, rows].astype(jnp.float32)
        beyond = pltpu.roll(xr[rows].astype(jnp.float32), nx - 2, 1)
        sides_of = jnp.where(lax.rem(lane, 2) == 0, xl[rows].astype(jnp.float32), beyond)

        def layer(z, state):
            previous, v, total, red, green, blue = state
            after = vf[z + 2, inner]
            near = vf.at[z + 1, pl.ds(r0, each + 16)]
            dz = after - previous
            dyv = near[pl.ds(9, each)] - near[pl.ds(7, each)]
            beside = pltpu.roll(sides_of, lax.rem(nx - 2 * z, nx), 1)
            right = jnp.where(lane == nx - 1, beside, pltpu.roll(v, nx - 1, 1))
            dxv = right - jnp.where(lane == 0, beside, pltpu.roll(v, 1, 1))
            lit = jnp.abs(dxv + 1.25 * dyv + (0.224 / 0.168) * dz)
            shade = (0.15 / 0.168) + lit * lax.rsqrt(dxv * dxv + dyv * dyv + dz * dz + 4.0)
            weight = share[z, rows] * shade
            tints = [jnp.tanh(v * slopes[i] + offsets[i]) for i in range(3)]
            return (
                v, after, total + weight,
                red + weight * tints[0], green + weight * tints[1], blue + weight * tints[2],
            )

        zero = jnp.zeros((each, nx), jnp.float32)
        state = (vb[0, rows].astype(jnp.float32), vf[1, inner], zero, zero, zero, zero)
        _, _, total, red, green, blue = lax.fori_loop(0, samples, layer, state, unroll=UNROLL)
        per = (LEVELS * 0.168) / jnp.maximum(decode(hide[j]), 1e-30)
        for i, value in enumerate((red, green, blue)):
            part[j, i] = to_level((value + total) * per)

    def veil(j):
        slot = slot_of(j)
        wait_from(hide, hides, hide_send, hide_recv, j)
        hidden = [decode(hides[s, slot]) for s in range(n)]
        top = hidden[0]
        for s in range(1, n):
            top = top + hidden[s] * (1.0 - top)
        code = encode(top)
        out[3, rows_of(j)] = code
        per = 1.0 / jnp.maximum(decode(code), 1e-30)
        for s in range(n):
            weight = hidden[s] * per
            for a in range(n):
                if a != s:
                    weight = weight * (1.0 - hidden[a] * before[a][s])
            factor[slot, s] = weight

    def merge(j):
        slot = slot_of(j)
        wait_from(part, parts, part_send, part_recv, j)
        for i in range(3):
            level = from_level(parts[0, slot, i]) * factor[slot, 0]
            for s in range(1, n):
                level = level + from_level(parts[s, slot, i]) * factor[slot, s]
            out[i, rows_of(j)] = to_level(level)

    def owned(j, act):
        pl.when((j >= 0) & (j < last_chunk) & (owner_of(j) == me))(act)

    def veil_owned(j):
        veil(j)
        spread(top_copy, j, lambda c: c.start())

    def merge_owned(j):
        merge(j)
        spread(fin_copy, j, lambda c: c.start())

    @pl.loop(0, last_chunk + RELAY_LAG)
    def _(i):
        @pl.when(i < chunks)
        def _():
            render(i)

            @pl.when(i == 0)
            def _():
                for r in range(max(3, n // 2 + 1), n):
                    far_wait(r)
                send_to_all(hide_copy, hide, hides)

            pl.when(i < last_chunk)(lambda: send_to_merger(part_copy, part, parts, i))
            pl.when(i == last_chunk)(lambda: send_to_all(part_copy, part, parts))

        for offset in range(2):
            j = 2 * (i - HIDE_LAG) + offset
            owned(j, functools.partial(veil_owned, j))
        pl.when(i == last_chunk)(lambda: veil(last_chunk))
        owned(i - MERGE_LAG, lambda: merge_owned(i - MERGE_LAG))
        pl.when(i == last_chunk + MERGE_LAG)(lambda: merge(last_chunk))
        j = i - RELAY_LAG

        @pl.when((j >= 0) & (j < last_chunk))
        def _():
            relay(top_copy, j)
            relay(fin_copy, j)

    for entry in halos:
        wait_sent(entry)
    for g in range(chunks // 2):
        for entry in edge_copies(g):
            wait_sent(entry)

    @pl.loop(0, last_chunk)
    def _(j):
        @pl.when(owner_of(j) != me)
        def _():
            hide_copy(j, owner_of(j)).wait_send()
            part_copy(j, owner_of(j)).wait_send()

        spread(top_copy, j, lambda c: c.wait_send())
        spread(fin_copy, j, lambda c: c.wait_send())

    for rel in range(1, n):
        hide_copy(last_chunk, lax.rem(me + rel, n)).wait_send()
        part_copy(last_chunk, lax.rem(me + rel, n)).wait_send()


def solution(mesh):
    n, n_tx, n_ty = mesh.shape["depth"], mesh.shape["tx"], mesh.shape["ty"]

    def shards(volume, transfer, ray_start, ray_stop, pattern, depth_order):
        samples, ny, nx = volume.shape
        rows = min(32, ny // 4)
        chunks = ny // rows
        slots = chunks - 1 - (chunks - 1) // 2 + 1
        f32, bf16, i16 = jnp.float32, jnp.bfloat16, jnp.int16
        any_space = pl.BlockSpec(memory_space=pl.ANY)
        smem = pl.BlockSpec(memory_space=pltpu.SMEM)
        dma = pltpu.SemaphoreType.DMA
        codes = pl.pallas_call(
            functools.partial(kernel, n, n_tx, n_ty, 2.0 / (samples * n), rows),
            out_shape=jax.ShapeDtypeStruct((4, ny, nx), i16),
            in_specs=[any_space, any_space, any_space, smem, smem, smem],
            out_specs=pl.BlockSpec(memory_space=pltpu.VMEM),
            scratch_shapes=[
                pltpu.VMEM((samples + 2, ny, nx), bf16),
                pltpu.VMEM((ny, nx), jnp.int32),
                pltpu.VMEM((ny, nx), jnp.int32),
                pltpu.VMEM((samples, STRIP, nx), bf16),
                pltpu.VMEM((samples, STRIP, nx), bf16),
                pltpu.VMEM((ny, nx), bf16),
                pltpu.VMEM((ny, nx), bf16),
                pltpu.VMEM((ny, nx), bf16),
                pltpu.VMEM((samples + 2, ny + 16, nx), f32),
                pltpu.VMEM((samples, ny, nx), f32),
                pltpu.VMEM((chunks, rows, nx), i16),
                pltpu.VMEM((n, slots, rows, nx), i16),
                pltpu.VMEM((chunks, 3, rows, nx), i16),
                pltpu.VMEM((n, slots, 3, rows, nx), i16),
                pltpu.VMEM((slots, n, rows, nx), f32),
                dma((chunks + 2,)), dma((4,)), dma((4,)), dma((chunks,)), dma((chunks,)),
                pltpu.SemaphoreType.REGULAR((n, 2)),
                dma((chunks, n)), dma((n, slots)), dma((chunks, n)), dma((n, slots)),
                dma((chunks, 2)), dma((chunks,)), dma((chunks, 2)), dma((chunks,)),
            ],
            compiler_params=pltpu.CompilerParams(
                collective_id=0, has_side_effects=True, vmem_limit_bytes=62 * 1024 * 1024
            ),
        )(volume, ray_start, ray_stop, pattern[:, :, 0], transfer.T, depth_order)
        top = decode(codes[3])
        colors = from_level(codes[:3]) * (top * (1.0 / LEVELS))
        return jnp.concatenate([colors, top[None]], axis=0)

    in_specs = (
        P("depth", "ty", "tx"),
        P(),
        P("depth", "ty", "tx"),
        P("depth", "ty", "tx"),
        P("depth", "ty", "tx"),
        P(),
    )
    return jax.shard_map(shards, mesh=mesh, in_specs=in_specs, out_specs=P(None, "ty", "tx"), check_vma=False)
```

time: 28.1 us -> 30.1 us (1.071)
  Pallas kernels: 26 us -> 27.2 us
  other arithmetic: 1.92 us -> 2.73 us
    select_n x1 -> x0, other arithmetic: 1.92 us -> none  [decode(): return jnp.where(wide == -32768, 0.0, value)]
    mul x0 -> x2, other arithmetic: none -> 1.9 us  [shards(): colors = from_level(codes[:3]) * (top * (1.0 / LEVELS))]
    pallas_call x1, Pallas kernels: 26 us -> 27.2 us  [shards(): pl.pallas_call(functools.partial(kernel, n, n_tx, n_ty, 2.0 / (samples *...]
    concatenate x0 -> x1, other arithmetic: none -> 0.83 us  [shards(): return jnp.concatenate([colors, top[None]], axis=0)]
where the time goes in v1:
time: 30.1 us; the launch traced here: 29.9 us
  Pallas kernels  27.2 us (90%)
  other arithmetic  2.73 us (9%)
    pallas_call x1, Pallas kernels, shards(): pl.pallas_call(functools.partial(kernel, n, n_tx, n_ty, 2.0 / (samples *...  27.2 us
    mul x2, other arithmetic, shards(): colors = from_level(codes[:3]) * (top * (1.0 / LEVELS))  1.9 us
    concatenate x1, other arithmetic, shards(): return jnp.concatenate([colors, top[None]], axis=0)  0.83 us

profile of v1, /device:TPU:0, one launch (start us, length us, event | category | flops | bytes accessed | tf_op | source)
XLA Modules:
  0.0 29.9 jit_solution(11908614733068104333)
XLA Ops:
  0.0 27.2 %shard_map.64 = s16[4,256,128]{2,1,0:T(8,128)(2,1)} custom-call(bf16[32,256,128]{2,1,0:T(8,128)(2,1)} %vol.1, s32[1,256,128]{2,1,0:T(8,128)} %start_hbm.1, s32[1,256,128]{2,1,0:T(8,128)} %stop_hbm.1, s32[1,32]{1,0:T(1,128)} %bitcast.5, f32[2,4]{1,0:T(2,128)} %bitcast.4, s32[4]{0:T(128)} %order.1), custom_call_target="tpu_custom_call" | custom-call | tf_op jit(solution)/shard_map/pallas_call | solution.py:430
  27.2 0.9 %multiply_bitcast_fusion = (f32[256,128]{1,0:T(8,128)S(1)}, f32[1,256,128]{2,1,0:T(8,128)S(1)}) fusion(s16[4,256,128]{2,1,0:T(8,128)(2,1)} %shard_map.64), kind=kLoop, calls=%fused_computation.8 | loop fusion | flops 229376 | bytes 327680 | tf_op jit(solution)/shard_map/mul | solution.py:461
  28.1 1.0 %add_multiply_fusion = f32[3,256,128]{2,1,0:T(8,128)S(1)} fusion(f32[256,128]{1,0:T(8,128)S(1)} %get-tuple-element.5, s16[4,256,128]{2,1,0:T(8,128)(2,1)} %shard_map.64), kind=kLoop, calls=%fused_computation.1 | loop fusion | flops 393216 | bytes 720896 | tf_op jit(solution)/shard_map/mul | solution.py:461
  29.1 0.8 %pad_maximum_fusion = f32[4,256,128]{2,1,0:T(8,128)} fusion(f32[1,256,128]{2,1,0:T(8,128)S(1)} %get-tuple-element.6, f32[3,256,128]{2,1,0:T(8,128)S(1)} %add_multiply_fusion), kind=kLoop, calls=%fused_computation | loop fusion | flops 131072 | bytes 1048576 | tf_op jit(solution)/shard_map/concatenate | solution.py:462

commit v2 on v1

--- a/solution.py
+++ b/solution.py
@@ -15,9 +15,8 @@
 OCTAVES = 24
 CODES = 65535.0 / OCTAVES
 LEVELS = 65000.0
-MERGE_LAG = 4
-RELAY_LAG = 7
-HIDE_LAG = 3
+VEIL_LAG = 4
+MERGE_LAG = 6
 
 
 def encode(x):
@@ -44,25 +43,21 @@
     vol, start_hbm, stop_hbm, pattern, transfer, order, out,
     vb, start, stop, yup, ydn, edge, xl, xr, vf, share,
     hide, hides, part, parts, factor,
-    load_sem, halo_send, halo_recv, edge_send, edge_recv, far,
+    load_sem, halo_send, halo_recv, deep_send, deep_recv, edge_send, edge_recv, far,
     hide_send, hide_recv, part_send, part_recv, fin_send, fin_recv, top_send, top_recv,
 ):
     samples, ny, nx = vol.shape
     chunks = ny // each
     group = 2 * each
-    last_chunk = chunks - 1
-    second = last_chunk // 2
-    slots = last_chunk - second + 1
+    groups = chunks // 2
+    mergers = (n // 2 - 1, n // 2)
     tx, ty, me = lax.axis_index("tx"), lax.axis_index("ty"), lax.axis_index("depth")
 
     def rows_of(j):
         return pl.ds(pl.multiple_of(j * each, each), each)
 
-    def owner_of(j):
-        return jnp.where(j < second, n // 2, n // 2 - 1)
-
-    def slot_of(j):
-        return jnp.where(j < second, j, jnp.where(j == last_chunk, slots - 1, j - second))
+    def group_of(g):
+        return pl.ds(pl.multiple_of(g * group, group), group)
 
     def load_piece(j):
         return pltpu.make_async_copy(
@@ -124,11 +119,17 @@
     halo = (halo_send, halo_recv)
     last, first = pl.ds(ny - STRIP, STRIP), pl.ds(0, STRIP)
     halos = [
-        (shift(halo, 2, "ty", ty, vol.at[:, last], yup, True), ty, n_ty, True, lambda: yup),
-        (shift(halo, 3, "ty", ty, vol.at[:, first], ydn, False), ty, n_ty, False, lambda: ydn),
-        (shift(halo, 0, "depth", me, vol.at[samples - 1], vb.at[0], True), me, n, True, lambda: vb.at[0]),
-        (shift(halo, 1, "depth", me, vol.at[0], vb.at[samples + 1], False), me, n, False, lambda: vb.at[samples + 1]),
+        (shift(halo, 0, "ty", ty, vol.at[:, last], yup, True), ty, n_ty, True, lambda: yup),
+        (shift(halo, 1, "ty", ty, vol.at[:, first], ydn, False), ty, n_ty, False, lambda: ydn),
     ]
+
+    def deep_copies(g):
+        rows = group_of(g)
+        sems = (deep_send, deep_recv)
+        return [
+            (shift(sems, 2 * g, "depth", me, vol.at[samples - 1, rows], vb.at[0, rows], True), me, n, True, None),
+            (shift(sems, 2 * g + 1, "depth", me, vol.at[0, rows], vb.at[samples + 1, rows], False), me, n, False, None),
+        ]
 
     def edge_copies(g):
         rows = pl.ds(pl.multiple_of(g * group, group), group)
@@ -154,13 +155,18 @@
         copy, at, count, upward, _ = entry
         pl.when(at > 0 if upward else at < count - 1)(copy.wait_recv)
 
+    for g in range(groups):
+        for entry in deep_copies(g):
+            send_halo(entry)
     for entry in halos:
         send_halo(entry)
     if n > 2:
         far_signal(2)
 
-    for at, count, place in ((tx, 0, xl), (tx, n_tx - 1, xr)):
-        @pl.when(at == count)
+    for at, edge_at, place in (
+        (tx, 0, xl), (tx, n_tx - 1, xr), (me, 0, vb.at[0]), (me, n - 1, vb.at[samples + 1]),
+    ):
+        @pl.when(at == edge_at)
         def _(place=place):
             place[...] = jnp.zeros(place.shape, jnp.bfloat16)
 
@@ -173,6 +179,45 @@
     before = [[jnp.where(rank[a] < rank[b], 1.0, 0.0) for b in range(n)] for a in range(n)]
     lane = lax.broadcasted_iota(jnp.int32, (each, nx), 1)
     pair = lax.shift_right_arithmetic(lane, 1)
+
+    merging = (me == mergers[0]) | (me == mergers[1])
+    handing = (me > 0) & (me < n - 1)
+    hide_refs = (hide, hides, hide_send, hide_recv, 2)
+    part_refs = (part, parts, part_send, part_recv, 1)
+
+    def to_merger(source, target, sends, recvs, count, j, origin, which):
+        block = pl.ds(j * count, count)
+        return pltpu.make_async_remote_copy(
+            src_ref=source.at[block], dst_ref=target.at[origin, block],
+            send_sem=sends.at[j, which], recv_sem=recvs.at[origin, j],
+            device_id={"depth": mergers[which]}, device_id_type=MESH,
+        )
+
+    def send_to_mergers(refs, j):
+        for which, merger in enumerate(mergers):
+            pl.when(me != merger)(lambda: to_merger(*refs, j, me, which).start())
+
+        @pl.when(merging)
+        def _():
+            for c in range(refs[4]):
+                refs[1][me, j * refs[4] + c] = refs[0][j * refs[4] + c]
+
+    def wait_parts(refs, j):
+        for s in range(n):
+            pl.when(me != s)(lambda: to_merger(*refs, j, s, 0).wait_recv())
+
+    def outward(block, sems, j):
+        return pltpu.make_async_remote_copy(
+            src_ref=out.at[block, rows_of(j)], dst_ref=out.at[block, rows_of(j)],
+            send_sem=sems[0].at[j], recv_sem=sems[1].at[j],
+            device_id={"depth": jnp.where(me < n // 2, me - 1, me + 1)}, device_id_type=MESH,
+        )
+
+    def top_copy(j):
+        return outward(3, (top_send, top_recv), j)
+
+    def fin_copy(j):
+        return outward(pl.ds(0, 3), (fin_send, fin_recv), j)
 
     for load in loads:
         load.wait()
@@ -212,76 +257,15 @@
             for entry in edge_copies(j // 2):
                 send_halo(entry)
 
-    def to_merger(source, target, sends, recvs, j, dest):
-        return pltpu.make_async_remote_copy(
-            src_ref=source.at[j], dst_ref=target.at[me, slot_of(j)],
-            send_sem=sends.at[j, lax.rem(dest + n - me, n)], recv_sem=recvs.at[me, slot_of(j)],
-            device_id={"depth": dest}, device_id_type=MESH,
-        )
-
-    def hide_copy(j, dest):
-        return to_merger(hide, hides, hide_send, hide_recv, j, dest)
-
-    def part_copy(j, dest):
-        return to_merger(part, parts, part_send, part_recv, j, dest)
-
-    def wait_from(source, target, sends, recvs, j):
-        for rel in range(1, n):
-            other = lax.rem(me + rel, n)
-            pltpu.make_async_remote_copy(
-                src_ref=source.at[j], dst_ref=target.at[other, slot_of(j)],
-                send_sem=sends.at[j, rel], recv_sem=recvs.at[other, slot_of(j)],
-                device_id={"depth": other}, device_id_type=MESH,
-            ).wait_recv()
-
-    def send_to_merger(copy, source, target, j):
-        owner = owner_of(j)
-
-        @pl.when(owner == me)
-        def _():
-            target[me, slot_of(j)] = source[j]
-
-        @pl.when(owner != me)
-        def _():
-            copy(j, owner).start()
-
-    def send_to_all(copy, source, target):
-        target[me, slots - 1] = source[last_chunk]
-        for rel in range(1, n):
-            copy(last_chunk, lax.rem(me + rel, n)).start()
-
-    def top_copy(j, right):
-        return pltpu.make_async_remote_copy(
-            src_ref=out.at[3, rows_of(j)], dst_ref=out.at[3, rows_of(j)],
-            send_sem=top_send.at[j, 1 if right else 0], recv_sem=top_recv.at[j],
-            device_id={"depth": me + 1 if right else me - 1}, device_id_type=MESH,
-        )
-
-    def fin_copy(j, right):
-        return pltpu.make_async_remote_copy(
-            src_ref=out.at[pl.ds(0, 3), rows_of(j)], dst_ref=out.at[pl.ds(0, 3), rows_of(j)],
-            send_sem=fin_send.at[j, 1 if right else 0], recv_sem=fin_recv.at[j],
-            device_id={"depth": me + 1 if right else me - 1}, device_id_type=MESH,
-        )
-
-    def spread(copy, j, act):
-        owner = owner_of(j)
-        pl.when((me >= owner) & (me < n - 1))(lambda: act(copy(j, True)))
-        pl.when((me <= owner) & (me > 0))(lambda: act(copy(j, False)))
-
-    def relay(copy, j):
-        @pl.when(owner_of(j) != me)
-        def _():
-            copy(j, True).wait_recv()
-            spread(copy, j, lambda c: c.start())
-
-    for r in range(2, max(3, n // 2 + 1)):
-        if r < n:
-            far_wait(r)
-
-    @pl.loop(0, last_chunk)
-    def _(j):
-        send_to_merger(hide_copy, hide, hides, j)
+            @pl.when(j == 1)
+            def _():
+                for r in range(2, max(3, n // 2 + 1)):
+                    far_wait(r)
+
+            send_to_mergers(hide_refs, j // 2)
+
+    for r in range(max(3, n // 2 + 1), n):
+        far_wait(r)
 
     for entry in halos:
         wait_arrived(entry)
@@ -297,7 +281,7 @@
 
         @pl.when(lax.rem(j, 2) == 0)
         def _():
-            for entry in edge_copies(j // 2):
+            for entry in edge_copies(j // 2) + deep_copies(j // 2):
                 wait_arrived(entry)
 
         vf[samples + 1, inner] = vb[samples + 1, rows].astype(jnp.float32)
@@ -330,89 +314,75 @@
             part[j, i] = to_level((value + total) * per)
 
     def veil(j):
-        slot = slot_of(j)
-        wait_from(hide, hides, hide_send, hide_recv, j)
-        hidden = [decode(hides[s, slot]) for s in range(n)]
+        hidden = [decode(hides[s, j]) for s in range(n)]
         top = hidden[0]
         for s in range(1, n):
             top = top + hidden[s] * (1.0 - top)
-        code = encode(top)
-        out[3, rows_of(j)] = code
-        per = 1.0 / jnp.maximum(decode(code), 1e-30)
+        out[3, rows_of(j)] = encode(top)
+        pl.when(handing)(lambda: top_copy(j).start())
         for s in range(n):
-            weight = hidden[s] * per
+            weight = hidden[s] * (1.0 / LEVELS)
             for a in range(n):
                 if a != s:
                     weight = weight * (1.0 - hidden[a] * before[a][s])
-            factor[slot, s] = weight
+            factor[j, s] = weight
 
     def merge(j):
-        slot = slot_of(j)
-        wait_from(part, parts, part_send, part_recv, j)
+        wait_parts(part_refs, j)
         for i in range(3):
-            level = from_level(parts[0, slot, i]) * factor[slot, 0]
+            color = from_level(parts[0, j, i]) * factor[j, 0]
             for s in range(1, n):
-                level = level + from_level(parts[s, slot, i]) * factor[slot, s]
-            out[i, rows_of(j)] = to_level(level)
-
-    def owned(j, act):
-        pl.when((j >= 0) & (j < last_chunk) & (owner_of(j) == me))(act)
-
-    def veil_owned(j):
-        veil(j)
-        spread(top_copy, j, lambda c: c.start())
-
-    def merge_owned(j):
-        merge(j)
-        spread(fin_copy, j, lambda c: c.start())
-
-    @pl.loop(0, last_chunk + RELAY_LAG)
+                color = color + from_level(parts[s, j, i]) * factor[j, s]
+            out[i, rows_of(j)] = encode(color)
+        pl.when(handing)(lambda: fin_copy(j).start())
+
+    @pl.loop(0, chunks + MERGE_LAG)
     def _(i):
         @pl.when(i < chunks)
         def _():
             render(i)
-
-            @pl.when(i == 0)
+            send_to_mergers(part_refs, i)
+
+        g = i - VEIL_LAG
+
+        @pl.when(merging & (g >= 0) & (g < groups))
+        def _():
+            wait_parts(hide_refs, g)
+            veil(2 * g)
+            veil(2 * g + 1)
+
+        pl.when(merging & (i >= MERGE_LAG))(lambda: merge(i - MERGE_LAG))
+
+    for copy in (top_copy, fin_copy):
+        @pl.loop(0, chunks)
+        def _(j, copy=copy):
+            @pl.when(jnp.logical_not(merging))
             def _():
-                for r in range(max(3, n // 2 + 1), n):
-                    far_wait(r)
-                send_to_all(hide_copy, hide, hides)
-
-            pl.when(i < last_chunk)(lambda: send_to_merger(part_copy, part, parts, i))
-            pl.when(i == last_chunk)(lambda: send_to_all(part_copy, part, parts))
-
-        for offset in range(2):
-            j = 2 * (i - HIDE_LAG) + offset
-            owned(j, functools.partial(veil_owned, j))
-        pl.when(i == last_chunk)(lambda: veil(last_chunk))
-        owned(i - MERGE_LAG, lambda: merge_owned(i - MERGE_LAG))
-        pl.when(i == last_chunk + MERGE_LAG)(lambda: merge(last_chunk))
-        j = i - RELAY_LAG
-
-        @pl.when((j >= 0) & (j < last_chunk))
-        def _():
-            relay(top_copy, j)
-            relay(fin_copy, j)
+                copy(j).wait_recv()
+                pl.when(handing)(lambda: copy(j).start())
 
     for entry in halos:
         wait_sent(entry)
-    for g in range(chunks // 2):
-        for entry in edge_copies(g):
+
+    @pl.loop(0, groups)
+    def _(g):
+        for entry in edge_copies(g) + deep_copies(g):
             wait_sent(entry)
 
-    @pl.loop(0, last_chunk)
+    @pl.loop(0, chunks)
     def _(j):
-        @pl.when(owner_of(j) != me)
-        def _():
-            hide_copy(j, owner_of(j)).wait_send()
-            part_copy(j, owner_of(j)).wait_send()
-
-        spread(top_copy, j, lambda c: c.wait_send())
-        spread(fin_copy, j, lambda c: c.wait_send())
-
-    for rel in range(1, n):
-        hide_copy(last_chunk, lax.rem(me + rel, n)).wait_send()
-        part_copy(last_chunk, lax.rem(me + rel, n)).wait_send()
+        for which, merger in enumerate(mergers):
+            pl.when(me != merger)(lambda: to_merger(*part_refs, j, me, which).wait_send())
+
+        @pl.when(handing)
+        def _():
+            top_copy(j).wait_send()
+            fin_copy(j).wait_send()
+
+    @pl.loop(0, groups)
+    def _(g):
+        for which, merger in enumerate(mergers):
+            pl.when(me != merger)(lambda: to_merger(*hide_refs, g, me, which).wait_send())
 
 
 def solution(mesh):
@@ -422,7 +392,6 @@
         samples, ny, nx = volume.shape
         rows = min(32, ny // 4)
         chunks = ny // rows
-        slots = chunks - 1 - (chunks - 1) // 2 + 1
         f32, bf16, i16 = jnp.float32, jnp.bfloat16, jnp.int16
         any_space = pl.BlockSpec(memory_space=pl.ANY)
         smem = pl.BlockSpec(memory_space=pltpu.SMEM)
@@ -444,22 +413,21 @@
                 pltpu.VMEM((samples + 2, ny + 16, nx), f32),
                 pltpu.VMEM((samples, ny, nx), f32),
                 pltpu.VMEM((chunks, rows, nx), i16),
-                pltpu.VMEM((n, slots, rows, nx), i16),
+                pltpu.VMEM((n, chunks, rows, nx), i16),
                 pltpu.VMEM((chunks, 3, rows, nx), i16),
-                pltpu.VMEM((n, slots, 3, rows, nx), i16),
-                pltpu.VMEM((slots, n, rows, nx), f32),
-                dma((chunks + 2,)), dma((4,)), dma((4,)), dma((chunks,)), dma((chunks,)),
+                pltpu.VMEM((n, chunks, 3, rows, nx), i16),
+                pltpu.VMEM((chunks, n, rows, nx), f32),
+                dma((chunks + 2,)), dma((2,)), dma((2,)),
+                dma((chunks,)), dma((chunks,)), dma((chunks,)), dma((chunks,)),
                 pltpu.SemaphoreType.REGULAR((n, 2)),
-                dma((chunks, n)), dma((n, slots)), dma((chunks, n)), dma((n, slots)),
-                dma((chunks, 2)), dma((chunks,)), dma((chunks, 2)), dma((chunks,)),
+                dma((chunks // 2, 2)), dma((n, chunks // 2)), dma((chunks, 2)), dma((n, chunks)),
+                dma((chunks,)), dma((chunks,)), dma((chunks,)), dma((chunks,)),
             ],
             compiler_params=pltpu.CompilerParams(
                 collective_id=0, has_side_effects=True, vmem_limit_bytes=62 * 1024 * 1024
             ),
         )(volume, ray_start, ray_stop, pattern[:, :, 0], transfer.T, depth_order)
-        top = decode(codes[3])
-        colors = from_level(codes[:3]) * (top * (1.0 / LEVELS))
-        return jnp.concatenate([colors, top[None]], axis=0)
+        return decode(codes)
 
     in_specs = (
         P("depth", "ty", "tx"),

time: 30.1 us -> 27.3 us (0.907)
  Pallas kernels: 27.2 us -> 25.2 us
  other arithmetic: 2.73 us -> 1.92 us
    select_n x0 -> x1, other arithmetic: none -> 1.92 us  [decode(): return jnp.where(wide == -32768, 0.0, value)]
    pallas_call x1, Pallas kernels: 27.2 us -> 25.2 us  [shards(): pl.pallas_call(functools.partial(kernel, n, n_tx, n_ty, 2.0 / (samples *...]
    mul x2 -> x0, other arithmetic: 1.9 us -> none  [shards(): colors = from_level(codes[:3]) * (top * (1.0 / LEVELS))]
    concatenate x1 -> x0, other arithmetic: 0.83 us -> none  [shards(): return jnp.concatenate([colors, top[None]], axis=0)]
where the time goes in v2:
time: 27.3 us; the launch traced here: 27.2 us
  Pallas kernels  25.2 us (92%)
  other arithmetic  1.92 us (7%)
    pallas_call x1, Pallas kernels, shards(): pl.pallas_call(functools.partial(kernel, n, n_tx, n_ty, 2.0 / (samples *...  25.2 us
    select_n x1, other arithmetic, decode(): return jnp.where(wide == -32768, 0.0, value)  1.92 us

profile of v2, /device:TPU:0, one launch (start us, length us, event | category | flops | bytes accessed | tf_op | source)
XLA Modules:
  0.0 27.2 jit_solution(3952116684051628836)
XLA Ops:
  0.0 25.2 %shard_map.64 = s16[4,256,128]{2,1,0:T(8,128)(2,1)} custom-call(bf16[32,256,128]{2,1,0:T(8,128)(2,1)} %vol.1, s32[1,256,128]{2,1,0:T(8,128)} %start_hbm.1, s32[1,256,128]{2,1,0:T(8,128)} %stop_hbm.1, s32[1,32]{1,0:T(1,128)} %bitcast.3, f32[2,4]{1,0:T(2,128)} %bitcast.2, s32[4]{0:T(128)} %order.1), custom_call_target="tpu_custom_call" | custom-call | tf_op jit(solution)/shard_map/pallas_call | solution.py:399
  25.3 1.9 %fusion.3 = f32[4,256,128]{2,1,0:T(8,128)} fusion(s16[4,256,128]{2,1,0:T(8,128)(2,1)} %shard_map.64), kind=kLoop, calls=%fused_computation.5 | loop fusion | flops 786432 | bytes 786432 | tf_op jit(solution)/shard_map/jit(_where)/select_n | solution.py:30

commit v3 on v2

--- a/solution.py
+++ b/solution.py
@@ -107,7 +107,7 @@
         def _():
             pl.semaphore_wait(far.at[r, 1], 1)
 
-        if r + 1 < n:
+        if r + 1 <= n // 2:
             far_signal(r + 1)
 
     def shift(sems, slot, axis, at, source, target, upward):
@@ -222,9 +222,23 @@
     for load in loads:
         load.wait()
 
+    def gather_edges(g):
+        for h in range(2):
+            load_piece(2 * g + h).wait()
+            rows = rows_of(2 * g + h)
+
+            def layer(z, edges):
+                v = vb[z + 1, rows].astype(jnp.float32)
+                return jnp.where(pair == z, pltpu.roll(v, lax.rem(2 * z + 1, nx), 1), edges)
+
+            edges = lax.fori_loop(0, samples, layer, jnp.zeros((each, nx), jnp.float32), unroll=UNROLL)
+            edge[rows] = edges.astype(jnp.bfloat16)
+        for entry in edge_copies(g):
+            send_halo(entry)
+
     @pl.loop(0, chunks)
     def _(j):
-        load_piece(j).wait()
+        pl.when(j < groups)(lambda: gather_edges(j))
         r0 = pl.multiple_of(j * each, each)
         rows, inner = rows_of(j), pl.ds(pl.multiple_of(r0 + 8, 8), each)
         begins, ends = [], []
@@ -235,37 +249,28 @@
             ends.append(jnp.where(on, stop[block], 0))
         begin, end = jnp.concatenate(begins, axis=0), jnp.concatenate(ends, axis=0)
 
-        def layer(early, z, state):
-            passed, edges = state
+        def layer(early, z, passed):
             v = vb[z + 1, rows].astype(jnp.float32)
             vf[z + 1, inner] = v
-            edges = jnp.where(pair == z, pltpu.roll(v, lax.rem(2 * z + 1, nx), 1), edges)
             log = jnp.log(1.0 + jnp.exp2(v * slope + offset))
             through = jnp.exp2(log * (-scale * LOG2E))
             now = jnp.where(begin <= z if early else end > z, passed * through, passed)
             share[z, rows] = passed - now
-            return now, edges
-
-        state = (jnp.ones((each, nx), jnp.float32), jnp.zeros((each, nx), jnp.float32))
+            return now
+
+        state = jnp.ones((each, nx), jnp.float32)
         state = lax.fori_loop(0, samples // 2, functools.partial(layer, True), state, unroll=UNROLL // 2)
-        passed, edges = lax.fori_loop(samples // 2, samples, functools.partial(layer, False), state, unroll=UNROLL // 2)
-        edge[rows] = edges.astype(jnp.bfloat16)
+        passed = lax.fori_loop(samples // 2, samples, functools.partial(layer, False), state, unroll=UNROLL // 2)
         hide[j] = encode(1.0 - passed)
 
         @pl.when(lax.rem(j, 2) == 1)
         def _():
-            for entry in edge_copies(j // 2):
-                send_halo(entry)
-
             @pl.when(j == 1)
             def _():
                 for r in range(2, max(3, n // 2 + 1)):
                     far_wait(r)
 
             send_to_mergers(hide_refs, j // 2)
-
-    for r in range(max(3, n // 2 + 1), n):
-        far_wait(r)
 
     for entry in halos:
         wait_arrived(entry)

time: 27.3 us -> 27.4 us (level)
  no operation moved by 1% of the time
where the time goes in v3:
time: 27.4 us; the launch traced here: 27.3 us
  Pallas kernels  25.3 us (92%)
  other arithmetic  1.92 us (7%)
    pallas_call x1, Pallas kernels, shards(): pl.pallas_call(functools.partial(kernel, n, n_tx, n_ty, 2.0 / (samples *...  25.3 us
    select_n x1, other arithmetic, decode(): return jnp.where(wide == -32768, 0.0, value)  1.92 us

profile of v3, /device:TPU:0, one launch (start us, length us, event | category | flops | bytes accessed | tf_op | source)
XLA Modules:
  0.0 27.3 jit_solution(7858996272782997479)
XLA Ops:
  0.0 25.3 %shard_map.64 = s16[4,256,128]{2,1,0:T(8,128)(2,1)} custom-call(bf16[32,256,128]{2,1,0:T(8,128)(2,1)} %vol.1, s32[1,256,128]{2,1,0:T(8,128)} %start_hbm.1, s32[1,256,128]{2,1,0:T(8,128)} %stop_hbm.1, s32[1,32]{1,0:T(1,128)} %bitcast.3, f32[2,4]{1,0:T(2,128)} %bitcast.2, s32[4]{0:T(128)} %order.1), custom_call_target="tpu_custom_call" | custom-call | tf_op jit(solution)/shard_map/pallas_call | solution.py:404
  25.3 1.9 %fusion.3 = f32[4,256,128]{2,1,0:T(8,128)} fusion(s16[4,256,128]{2,1,0:T(8,128)(2,1)} %shard_map.64), kind=kLoop, calls=%fused_computation.5 | loop fusion | flops 786432 | bytes 786432 | tf_op jit(solution)/shard_map/jit(_where)/select_n | solution.py:30

commit v4 on v2

--- a/solution.py
+++ b/solution.py
@@ -16,7 +16,7 @@
 CODES = 65535.0 / OCTAVES
 LEVELS = 65000.0
 VEIL_LAG = 4
-MERGE_LAG = 6
+MERGE_LAG = 5
 
 
 def encode(x):
@@ -107,7 +107,7 @@
         def _():
             pl.semaphore_wait(far.at[r, 1], 1)
 
-        if r + 1 < n:
+        if r + 1 <= n // 2:
             far_signal(r + 1)
 
     def shift(sems, slot, axis, at, source, target, upward):
@@ -263,9 +263,6 @@
                     far_wait(r)
 
             send_to_mergers(hide_refs, j // 2)
-
-    for r in range(max(3, n // 2 + 1), n):
-        far_wait(r)
 
     for entry in halos:
         wait_arrived(entry)

time: 27.3 us -> 27.3 us (level)
  no operation moved by 1% of the time
where the time goes in v4:
time: 27.3 us; the launch traced here: 27.2 us
  Pallas kernels  25.2 us (92%)
  other arithmetic  1.92 us (7%)
    pallas_call x1, Pallas kernels, shards(): pl.pallas_call(functools.partial(kernel, n, n_tx, n_ty, 2.0 / (samples *...  25.2 us
    select_n x1, other arithmetic, decode(): return jnp.where(wide == -32768, 0.0, value)  1.92 us

profile of v4, /device:TPU:0, one launch (start us, length us, event | category | flops | bytes accessed | tf_op | source)
XLA Modules:
  0.0 27.2 jit_solution(12690503789322820319)
XLA Ops:
  0.0 25.2 %shard_map.64 = s16[4,256,128]{2,1,0:T(8,128)(2,1)} custom-call(bf16[32,256,128]{2,1,0:T(8,128)(2,1)} %vol.1, s32[1,256,128]{2,1,0:T(8,128)} %start_hbm.1, s32[1,256,128]{2,1,0:T(8,128)} %stop_hbm.1, s32[1,32]{1,0:T(1,128)} %bitcast.3, f32[2,4]{1,0:T(2,128)} %bitcast.2, s32[4]{0:T(128)} %order.1), custom_call_target="tpu_custom_call" | custom-call | tf_op jit(solution)/shard_map/pallas_call | solution.py:396
  25.2 1.9 %fusion.3 = f32[4,256,128]{2,1,0:T(8,128)} fusion(s16[4,256,128]{2,1,0:T(8,128)(2,1)} %shard_map.64), kind=kLoop, calls=%fused_computation.5 | loop fusion | flops 786432 | bytes 786432 | tf_op jit(solution)/shard_map/jit(_where)/select_n | solution.py:30

commit v5 on v2

--- a/solution.py
+++ b/solution.py
@@ -427,7 +427,8 @@
                 collective_id=0, has_side_effects=True, vmem_limit_bytes=62 * 1024 * 1024
             ),
         )(volume, ray_start, ray_stop, pattern[:, :, 0], transfer.T, depth_order)
-        return decode(codes)
+        wide = codes.astype(f32)
+        return jnp.where(wide == -32768.0, 0.0, jnp.exp2((wide - 32767.0) * (1.0 / CODES)))
 
     in_specs = (
         P("depth", "ty", "tx"),

time: 27.3 us -> 27.3 us (level)
  no operation moved by 1% of the time
where the time goes in v5:
time: 27.3 us; the launch traced here: 27.2 us
  Pallas kernels  25.2 us (92%)
  other arithmetic  1.92 us (7%)
    pallas_call x1, Pallas kernels, shards(): pl.pallas_call(functools.partial(kernel, n, n_tx, n_ty, 2.0 / (samples *...  25.2 us
    select_n x1, other arithmetic, shards(): jnp.where(wide == -32768.0, 0.0, jnp.exp2((wide - 32767.0) * (1.0 / CODES)))  1.92 us

profile of v5, /device:TPU:0, one launch (start us, length us, event | category | flops | bytes accessed | tf_op | source)
XLA Modules:
  0.0 27.2 jit_solution(18047741132247897722)
XLA Ops:
  0.0 25.2 %shard_map.64 = s16[4,256,128]{2,1,0:T(8,128)(2,1)} custom-call(bf16[32,256,128]{2,1,0:T(8,128)(2,1)} %vol.1, s32[1,256,128]{2,1,0:T(8,128)} %start_hbm.1, s32[1,256,128]{2,1,0:T(8,128)} %stop_hbm.1, s32[1,32]{1,0:T(1,128)} %bitcast.3, f32[2,4]{1,0:T(2,128)} %bitcast.2, s32[4]{0:T(128)} %order.1), custom_call_target="tpu_custom_call" | custom-call | tf_op jit(solution)/shard_map/pallas_call | solution.py:399
  25.3 1.9 %fusion.2 = f32[4,256,128]{2,1,0:T(8,128)} fusion(s16[4,256,128]{2,1,0:T(8,128)(2,1)} %shard_map.64), kind=kLoop, calls=%fused_computation.4 | loop fusion | flops 655360 | bytes 786432 | tf_op jit(solution)/shard_map/jit(_where)/select_n | solution.py:431
